TPU v7x, 768 devices: a whole 4x8x12 slice. The times are simulated.
768 devices in a mesh: section: 8 (over x, core), seq: 32 (over z_lo, y), head: 3 (over z_hi).
Axes of the slice: x: 4, y: 8, z: 12 (z_hi: 3, z_lo: 4; z = z_hi * 4 + z_lo), core: 2. Of those that a mesh axis runs over, the one named last changes fastest.
Arguments:
- queries: bfloat16 [8, 4096, 2304], P('section', 'seq', 'head'), may hold values from -240 to 240
- grad_out: bfloat16 [8, 4096, 2304], P('section', 'seq', 'head'), may hold values from -96 to 96
- keys: bfloat16 [8, 2048, 1152], P('section', 'seq', 'head'), may hold values from -6 to 6
- values: bfloat16 [8, 2048, 1152], P('section', 'seq', 'head'), may hold values from -6 to 6
- proj_query: bfloat16 [8, 5376, 2304], P('section', None, 'head'), may hold values from -0.125 to 0.125
- section_span: int32 [8], replicated, may hold values from 0 to 7, each once
- span_prefix: int32 [8], replicated, may hold values from 1024 to 2048, as said below
Outputs:
- grad_input: bfloat16 [8, 5376, 4096], P('section', 'head', 'seq')
- grad_key: bfloat16 [8, 2048, 1152], P('section', 'seq', 'head')
- grad_value: bfloat16 [8, 2048, 1152], P('section', 'seq', 'head')
Inputs may be any that keep to these rules, and one draw needn't show every extreme that they name: `span_prefix`: some entry equals 2048 in every draw.
All inputs are finite; a program needn't handle non-finite values.
Results may differ from a plain program's by a relative error of at most 0.023.
Values may be sent and summed in bfloat16 or wider, within the bound.
A program may use at most 64 MiB of HBM per device.

v0:
```python
import jax
import jax.numpy as jnp
from jax import lax
from jax.sharding import Mesh
from jax.sharding import PartitionSpec as P

HD = 128
SEQ = ("seq_0", "seq_1")


query_scale = 168.0 ** (-0.5)


def shifted(block, axis, distance):
    devices = range(lax.axis_size(axis))
    route = [((i - distance) % len(devices), i) for i in devices]
    return lax.ppermute(block, axis, route)


def sent_together(arrays, axis, dim, along):
    ends, at = ([], 0)
    for a in arrays[:-1]:
        at += a.shape[along]
        ends.append(at)
    both = jnp.concatenate(arrays, axis=along)
    return tuple(jnp.split(lax.all_gather(both, axis, axis=dim, tiled=True), ends, axis=along))


def own_block(pieces, axes, order):
    shape = [lax.axis_size(a) for a in axes]
    pieces = pieces.reshape(*shape, *pieces.shape[1:])
    pieces = pieces.transpose(*order, *range(len(axes), pieces.ndim))
    pieces = pieces.reshape(-1, *pieces.shape[len(axes) :])
    for k in order:
        pieces = lax.psum_scatter(pieces, axes[k], scatter_dimension=0, tiled=True)
    return pieces[0]


def split_up(array, dim, length):
    before, after = (array.shape[:dim], array.shape[dim + 1 :])
    return jnp.moveaxis(array.reshape(*before, length, -1, *after), dim, 0)


def sum_by_axis_2(array, axes, order, dim):
    length = lax.axis_size(axes)
    return own_block(split_up(array, dim, length), axes, order)


def sum_at_owner(array, axis, dim):
    pieces = split_up(array, dim, lax.axis_size(axis))
    arrived = lax.all_to_all(pieces, axis, split_axis=0, concat_axis=0, tiled=True)
    return arrived.sum(axis=0)


def to_groups(matrix):
    count = matrix.shape[1] // (2 * HD)
    return (
        matrix.reshape(matrix.shape[0], count, 2, HD)
        .transpose(1, 2, 0, 3)
        .reshape(count, 2 * matrix.shape[0], HD)
    )


def from_groups(stacked):
    count = stacked.shape[0]
    rows_half = stacked.shape[1] // 2
    return (
        stacked.reshape(count, 2, rows_half, HD)
        .transpose(2, 0, 1, 3)
        .reshape(rows_half, count * 2 * HD)
    )


def kv_groups(matrix):
    return matrix.reshape(matrix.shape[0], matrix.shape[1] // HD, HD).transpose(1, 0, 2)


def kv_flat(stacked):
    return stacked.transpose(1, 0, 2).reshape(stacked.shape[1], stacked.shape[0] * HD)


def contract_rows(left, right):
    return lax.dot_general(
        left, right, (((0,), (0,)), ((), ())), preferred_element_type=jnp.float32
    )


def rounded(matrix):
    return lax.optimization_barrier(matrix.astype(jnp.bfloat16)).astype(jnp.float32)


def group_pass(q_group, d_group, k_group, v_group, live):
    scores = query_scale * jnp.dot(q_group, k_group.T, preferred_element_type=jnp.float32)
    scores = jnp.where(live[None, :], scores, jnp.float32(-1e30))
    top = jnp.max(scores, axis=1, keepdims=True)
    lse = top + jnp.log(jnp.sum(jnp.exp(scores - top), axis=1, keepdims=True))
    probs = jnp.where(live[None, :], jnp.exp(scores - lse), jnp.float32(0.0))
    probs_low = probs.astype(jnp.bfloat16)
    dprobs = jnp.dot(d_group, v_group.T, preferred_element_type=jnp.float32)
    attn = jnp.dot(probs_low, v_group, preferred_element_type=jnp.float32)
    delta = jnp.sum(d_group.astype(jnp.float32) * attn, axis=1, keepdims=True)
    dscores = (probs * (dprobs - delta)).astype(jnp.bfloat16)
    grad_q = (query_scale * jnp.dot(dscores, k_group, preferred_element_type=jnp.float32)).astype(
        jnp.bfloat16
    )
    grad_k = query_scale * contract_rows(dscores, q_group)
    grad_v = contract_rows(probs_low, d_group)
    return (grad_q, grad_k, grad_v, lse, delta)


def on_device(queries, grad_out, keys, values, proj_query, section_span, span_prefix):
    incoming = shifted(grad_out, "section", -1)
    key_all, value_all = sent_together((keys, values), SEQ, 1, 0)
    prefix = key_all.shape[1]
    length = span_prefix[section_span[lax.axis_index("section")]]
    live = jnp.arange(prefix, dtype=jnp.int32) < length
    q_groups = to_groups(queries[0])
    d_groups = to_groups(incoming[0])
    k_groups = kv_groups(key_all[0])
    v_groups = kv_groups(value_all[0])

    def per_group(members):
        return group_pass(members[0], members[1], members[2], members[3], live)

    grad_q, grad_k, grad_v, lse, delta = lax.map(
        per_group, (q_groups, d_groups, k_groups, v_groups)
    )
    grad_query = from_groups(grad_q)
    stored = rounded(jnp.concatenate([kv_flat(grad_k), kv_flat(grad_v)], axis=1))
    summed = sum_by_axis_2(stored.astype(jnp.bfloat16), SEQ, (1, 0), 0).astype(jnp.float32)
    half_cols = summed.shape[1] // 2
    grad_key = summed[:, :half_cols].astype(jnp.bfloat16)[None]
    grad_value = summed[:, half_cols:].astype(jnp.bfloat16)[None]
    weight = proj_query[0]
    grad_input = sum_at_owner(
        lax.dot_general(
            weight, grad_query, (((1,), (1,)), ((), ())), preferred_element_type=jnp.float32
        ),
        "head",
        0,
    )
    return (grad_input.astype(jnp.bfloat16)[None], grad_key, grad_value)


def solution(mesh):
    split = Mesh(
        mesh.devices.reshape(mesh.shape["section"], 4, 8, mesh.shape["head"]),
        ("section", "seq_0", "seq_1", "head"),
    )
    in_specs = (
        P("section", SEQ, "head"),
        P("section", SEQ, "head"),
        P("section", SEQ, "head"),
        P("section", SEQ, "head"),
        P("section", None, "head"),
        P(),
        P(),
    )
    out_specs = (P("section", "head", SEQ), P("section", SEQ, "head"), P("section", SEQ, "head"))
    return jax.shard_map(
        on_device, mesh=split, in_specs=in_specs, out_specs=out_specs, check_vma=False
    )
```

profile of v0, /device:TPU:1, one launch (start us, length us, event | category | flops | bytes accessed | tf_op | source)
XLA Modules:
  0.0 326.7 jit_solution(929168265559671060)
XLA Ops:
  9.9 10.5 %collective-permute-start = (bf16[1,128,768]{2,1,0:T(8,128)(2,1)}, bf16[1,128,768]{2,1,0:T(8,128)(2,1)S(1)}, u32[]{:S(2)}, u32[]{:S(2)}) collective-permute-start(bf16[1,128,768]{2,1,0:T(8,128)(2,1)} %param.10), channel_id=1, source_target_pairs={{96,0},{192,96},{288,192},{384,288},{480,384},{576,480},{672,576},... | collective-permute-start | bytes 589832 | tf_op jit(solution)/shard_map/ppermute | solution.py:17
  20.4 1.2 dynamic_slice.20
  24.6 1.2 dynamic_slice.21
  26.3 129.5 %all-gather.2.cloned.1.call-done = bf16[2,2048,384]{2,0,1:T(2,128)(2,1)} async-done(((bf16[2,64,384]{2,0,1:T(2,128)(2,1)}), bf16[2,2048,384]{2,0,1:T(2,128)(2,1)}) %all-gather.2.cloned.1.call-update) | async-done | bytes 3145744 | tf_op jit(solution)/shard_map/all_gather | solution.py:26
  155.8 8.6 %fusion.42 = (bf16[1,2048,384]{2,0,1:T(2,128)(2,1)S(1)}, bf16[1,2048,384]{2,0,1:T(2,128)(2,1)}) fusion(bf16[2,2048,384]{2,0,1:T(2,128)(2,1)} %all-gather.2.cloned.1.call-done), kind=kLoop, calls=%fused_computation.53 | loop fusion | bytes 6291456 | tf_op jit(solution)/shard_map/split | solution.py:26
  164.4 8.2 %copy.54 = bf16[1,2048,384]{1,2,0:T(8,128)(2,1)} copy(bf16[1,2048,384]{2,0,1:T(2,128)(2,1)} %get-tuple-element.124) | data formatting | bytes 3145728
  172.6 6.2 %copy.55 = bf16[1,2048,384]{1,2,0:T(8,128)(2,1)} copy(bf16[1,2048,384]{2,0,1:T(2,128)(2,1)S(1)} %get-tuple-element.123) | data formatting | bytes 3145728
  178.9 27.5 %while.15 = (s32[]{:T(128)}, bf16[3,256,128]{2,1,0:T(8,128)(2,1)}, bf16[3,2048,128]{1,2,0:T(8,128)(2,1)}, bf16[3,2048,128]{1,2,0:T(8,128)(2,1)}, bf16[3,256,128]...) while((s32[]{:T(128)}, bf16[3,256,128]{2,1,0:T(8,128)(2,1)}, ...), condition=%wide.region_4.5_spmd.clone, body=%wide.region_0.4_spmd.clone.sunk | while | flops 814384640 | bytes 38693568 | solution.py:125
  179.5 1.7 fusion.72
  185.9 2.1 fusion.75
  188.7 1.7 fusion.72
  195.1 2.1 fusion.75
  197.9 1.7 fusion.72
  204.2 2.1 fusion.75
  206.3 2.1 pad_maximum_fusion
  208.4 2.8 copy.46
  211.3 3.9 %copy.47 = bf16[8,4,64,768]{3,2,1,0:T(8,128)(2,1)} copy(bf16[8,4,64,768]{3,2,0,1:T(8,128)(2,1)} %bitcast.116) | data formatting | bytes 6291456 | tf_op jit(solution)/shard_map/transpose | solution.py:32
  216.3 6.1 %fusion.38 = f32[5376,128]{0,1:T(8,128)S(1)} fusion(bf16[128,768]{0,1:T(8,128)(2,1)S(1)} %bitcast.122, bf16[1,5376,768]{2,1,0:T(8,128)(2,1)} %param.13), kind=kOutput, calls=%fused_computation.46 | convolution fusion | flops 1056964608 | bytes 11206656 | tf_op jit(solution)/shard_map/dot_general | solution.py:136
  222.4 2.2 copy.43
  224.6 6.5 %all-to-all-start = ((f32[3,1792,128]{2,1,0:T(8,128)}), f32[3,1792,128]{2,1,0:T(8,128)S(1)}, u32[]{:S(2)}, u32[]{:S(2)}) async-start(f32[3,1792,128]{2,1,0:T(8,128)} %bitcast.118), calls=%async_computation | async-start | bytes 5505024 | tf_op jit(solution)/shard_map/all_to_all | solution.py:51
  231.1 51.4 %reduce-scatter.3.cloned.1.call-done = bf16[4,64,768]{2,1,0:T(8,128)(2,1)} async-done(((bf16[32,64,768]{2,1,0:T(8,128)(2,1)}), bf16[4,64,768]{2,1,0:T(8,128)(2,1)}) %reduce-scatter.3.cloned.1.call-update) | async-done | bytes 393232 | tf_op jit(solution)/shard_map/reduce_scatter | solution.py:35
  282.6 1.0 reduce_sum.27
  283.6 35.1 %reduce-scatter.5.cloned.1.call-done = bf16[1,64,768]{2,1,0:T(8,128)(2,1)} async-done(((bf16[4,64,768]{2,1,0:T(8,128)(2,1)}), bf16[1,64,768]{2,1,0:T(8,128)(2,1)}) %reduce-scatter.5.cloned.1.call-update) | async-done | bytes 98320 | tf_op jit(solution)/shard_map/reduce_scatter | solution.py:35
  318.7 1.5 slice_bitcast_fusion
  (67 shorter events, 21.0 us)
Async XLA Ops:
  7.2 148.6 %all-gather.2.cloned.1.call-start = ((), (), s32[]{:S(2)}) async-start(), calls=%async_computation.3 | async-start | bytes 3244032 | tf_op jit(solution)/shard_map/all_gather | solution.py:26
  9.9 272.7 %reduce-scatter.3.cloned.1.call-start = ((), (), s32[]{:S(2)}) async-start(), calls=%async_computation.4 | async-start | bytes 3538944 | tf_op jit(solution)/shard_map/reduce_scatter | solution.py:35
  9.9 16.0 %collective-permute-start = (bf16[1,128,768]{2,1,0:T(8,128)(2,1)}, bf16[1,128,768]{2,1,0:T(8,128)(2,1)S(1)}, u32[]{:S(2)}, u32[]{:S(2)}) collective-permute-start(bf16[1,128,768]{2,1,0:T(8,128)(2,1)} %param.10), channel_id=1, source_target_pairs={{96,0},{192,96},{288,192},{384,288},{480,384},{576,480},{672,576},... | collective-permute-start | bytes 589832 | tf_op jit(solution)/shard_map/ppermute | solution.py:17
  179.5 2.2 copy-start.1
  181.7 1.4 copy-start
  182.3 2.1 copy-start.2
  188.7 2.2 copy-start.1
  190.8 1.4 copy-start
  191.4 2.1 copy-start.2
  197.9 2.2 copy-start.1
  200.0 1.4 copy-start
  200.6 2.1 copy-start.2
  215.2 0.9 copy-start.3
  224.6 58.0 %all-to-all-start = ((f32[3,1792,128]{2,1,0:T(8,128)}), f32[3,1792,128]{2,1,0:T(8,128)S(1)}, u32[]{:S(2)}, u32[]{:S(2)}) async-start(f32[3,1792,128]{2,1,0:T(8,128)} %bitcast.118), calls=%async_computation | async-start | bytes 5505024 | tf_op jit(solution)/shard_map/all_to_all | solution.py:51
  231.1 87.6 %reduce-scatter.5.cloned.1.call-start = ((), (), s32[]{:S(2)}) async-start(), calls=%async_computation.5 | async-start | bytes 491520 | tf_op jit(solution)/shard_map/reduce_scatter | solution.py:35
Sparse Core Ops, SparseCore 0:
  10.3 145.3 all-gather.1
  215.3 67.1 reduce-scatter.2
  285.7 32.9 reduce-scatter.4
where the time goes:
time: 329 us; the launch traced here: 327 us
  waiting for transfers between devices  216 us (66%)
  local copies, waits for them, and re-layouts  45.7 us (14%)
  matrix products  24.5 us (7%)
  starting transfers between devices  17.1 us (5%)
  between operations  15.8 us (5%)
  other arithmetic  7.29 us (2%)
    all_gather x1, waiting for transfers between devices, sent_together(): lax.all_gather(both, axis, axis=dim, tiled=True)  130 us
    reduce_scatter x2, waiting for transfers between devices, own_block(): pieces = lax.psum_scatter(pieces, axes[k], scatter_dimension=0, tiled=True)  86.5 us
    unnamed x6, local copies, waits for them, and re-layouts  17.1 us
    ppermute x1, starting transfers between devices, shifted(): return lax.ppermute(block, axis, route)  10.5 us
    split x1, local copies, waits for them, and re-layouts, sent_together(): jnp.split(lax.all_gather(both, axis, axis=dim, tiled=True), ends, axis=al...  8.63 us
  transfers between devices with their start and end apart: 5, of which 3 were waited for; matrix products, arithmetic and copies ran while one was open for 4% of the time, Pallas kernels for 0%

commit v1 on v0

v1 whole, which is shorter than its diff:
```python
import functools
import math

import jax
import jax.numpy as jnp
from jax import lax
from jax.experimental import pallas as pl
from jax.experimental.pallas import tpu as pltpu
from jax.sharding import Mesh
from jax.sharding import PartitionSpec as P

HD = 128
SEQ = ("seq_0", "seq_1")
NZ = 4
NY = 8
SCALE = 168.0 ** (-0.5)
SCALE_LOG2 = SCALE * math.log2(math.e)
CHUNK = 256
VMEM = pltpu.VMEM
DMA = pltpu.SemaphoreType.DMA


def column_mates(z):
    return (z + 1 - 2 * (z % 2), (z + 2) % NZ, NZ - 1 - z)


def remote(src, dst, send, recv, target):
    return pltpu.make_async_remote_copy(
        src_ref=src,
        dst_ref=dst,
        send_sem=send,
        recv_sem=recv,
        device_id=target,
        device_id_type=pl.DeviceIdType.MESH,
    )


def greet(targets):
    barrier = pltpu.get_barrier_semaphore()
    for target in targets:
        pl.semaphore_signal(
            barrier, inc=1, device_id=target, device_id_type=pl.DeviceIdType.MESH
        )
    pl.semaphore_wait(barrier, len(targets))


def gather_kernel(k_ref, v_ref, d_ref, k_all, v_all, d_new, send, recv, shift_sem, own_sem):
    z = lax.axis_index("seq_0")
    y = lax.axis_index("seq_1")
    s = lax.axis_index("section")
    right, left = (y + 1) % NY, (y + NY - 1) % NY
    mates = column_mates(z)
    down, up = (s + 7) % 8, (s + 1) % 8
    greet(
        [{"seq_1": right}, {"seq_1": left}]
        + [{"seq_0": m} for m in mates]
        + [{"section": down}, {"section": up}]
    )
    own = (k_ref, v_ref)
    full = (k_all, v_all)
    sent = []

    def push(src, kv, z0, y0, target):
        copy = remote(src, full[kv].at[z0, y0], send.at[len(sent)], recv.at[kv, z0, y0], target)
        copy.start()
        sent.append(copy)

    def arrived(kv, z0, y0):
        block = full[kv].at[z0, y0]
        remote(block, block, send.at[0], recv.at[kv, z0, y0], {"seq_1": right}).wait_recv()

    for kv in range(2):
        for m in mates:
            push(own[kv], kv, z, y, {"seq_0": m})
    for kv in range(2):
        push(own[kv], kv, z, y, {"seq_1": right})
        push(own[kv], kv, z, y, {"seq_1": left})
    shift = remote(d_ref, d_new, shift_sem.at[0], shift_sem.at[1], {"section": down})
    shift.start()
    here = [pltpu.make_async_copy(own[kv], full[kv].at[z, y], own_sem.at[kv]) for kv in range(2)]
    for copy in here:
        copy.start()
    for m in mates:
        for kv in range(2):
            arrived(kv, m, y)
            push(full[kv].at[m, y], kv, m, y, {"seq_1": right})
            push(full[kv].at[m, y], kv, m, y, {"seq_1": left})
    reach = ((4, 3), (3, 4))
    for hop in range(1, 5):
        for m in (z,) + mates:
            for kv in range(2):
                if hop <= reach[kv][0]:
                    y0 = (y + NY - hop) % NY
                    arrived(kv, m, y0)
                    if hop < reach[kv][0]:
                        push(full[kv].at[m, y0], kv, m, y0, {"seq_1": right})
                if hop <= reach[kv][1]:
                    y0 = (y + hop) % NY
                    arrived(kv, m, y0)
                    if hop < reach[kv][1]:
                        push(full[kv].at[m, y0], kv, m, y0, {"seq_1": left})
    for copy in sent:
        copy.wait_send()
    for copy in here:
        copy.wait()
    shift.wait()


def gathered(k, v, d):
    count = 62
    return pl.pallas_call(
        gather_kernel,
        out_shape=(
            jax.ShapeDtypeStruct((NZ, NY) + k.shape, k.dtype),
            jax.ShapeDtypeStruct((NZ, NY) + v.shape, v.dtype),
            jax.ShapeDtypeStruct(d.shape, d.dtype),
        ),
        in_specs=[pl.BlockSpec(memory_space=VMEM)] * 3,
        out_specs=(pl.BlockSpec(memory_space=VMEM),) * 3,
        scratch_shapes=[DMA((count,)), DMA((2, NZ, NY)), DMA((2,)), DMA((2,))],
        compiler_params=pltpu.CompilerParams(collective_id=0, has_side_effects=True),
        name="gather_kv",
    )(k, v, d)


def dot_nt(a, b):
    return lax.dot_general(a, b, (((1,), (1,)), ((), ())), preferred_element_type=jnp.float32)


def dot_nn(a, b):
    return lax.dot_general(a, b, (((1,), (0,)), ((), ())), preferred_element_type=jnp.float32)


def dot_tn(a, b):
    return lax.dot_general(a, b, (((0,), (0,)), ((), ())), preferred_element_type=jnp.float32)


def by_eight(x):
    return x.reshape(x.shape[0] // 8, 8, x.shape[1])


def attention_kernel(len_ref, q_ref, d_ref, k_ref, v_ref, gq_ref, gk_ref, gv_ref, s_buf, p_buf):
    length = len_ref[0]
    prefix = k_ref.shape[0]
    two = lambda ref: jnp.concatenate([ref[:, :HD], ref[:, HD:]], axis=0)
    q2, d2 = two(q_ref), two(d_ref)
    cols = q2.shape[0]
    chunks = [pl.ds(at, CHUNK) for at in range(0, prefix, CHUNK)]
    top = jnp.full((8, cols), -1e30, jnp.float32)
    for c, rows in enumerate(chunks):
        s = dot_nt(k_ref[rows, :], q2)
        t = c * CHUNK + lax.broadcasted_iota(jnp.int32, s.shape, 0)
        s = jnp.where(t < length, s, jnp.float32(-1e30))
        s_buf[rows, :] = s
        top = jnp.maximum(top, by_eight(s).max(axis=0))
    top = top.max(axis=0, keepdims=True)
    total = jnp.zeros((8, cols), jnp.float32)
    dots = jnp.zeros((8, cols), jnp.float32)
    for rows in chunks:
        e = jnp.exp2((s_buf[rows, :] - top) * SCALE_LOG2)
        dp = dot_nt(v_ref[rows, :], d2)
        s_buf[rows, :] = e
        p_buf[rows, :] = dp
        total = total + by_eight(e).sum(axis=0)
        dots = dots + by_eight(e * dp).sum(axis=0)
    inv = 1.0 / total.sum(axis=0, keepdims=True)
    delta = dots.sum(axis=0, keepdims=True) * inv
    gq = jnp.zeros((HD, cols), jnp.float32)
    for rows in chunks:
        p = s_buf[rows, :] * inv
        ds = (p * (p_buf[rows, :] - delta)).astype(jnp.bfloat16)
        gv_ref[rows, :] = dot_nn(p.astype(jnp.bfloat16), d2).astype(jnp.bfloat16)
        gk_ref[rows, :] = (SCALE * dot_nn(ds, q2)).astype(jnp.bfloat16)
        gq = gq + dot_tn(k_ref[rows, :], ds)
    gq = (SCALE * gq).astype(jnp.bfloat16)
    half = cols // 2
    gq_ref[:HD, :] = gq[:, :half]
    gq_ref[HD:, :] = gq[:, half:]


def attention(length, q, d, k, v):
    rows, width = q.shape
    groups = width // (2 * HD)
    prefix = k.shape[0]
    row_spec = pl.BlockSpec((rows, 2 * HD), lambda g, n: (0, g))
    key_spec = pl.BlockSpec((prefix, HD), lambda g, n: (0, g))
    return pl.pallas_call(
        attention_kernel,
        out_shape=(
            jax.ShapeDtypeStruct((width, rows), jnp.bfloat16),
            jax.ShapeDtypeStruct(k.shape, jnp.bfloat16),
            jax.ShapeDtypeStruct(v.shape, jnp.bfloat16),
        ),
        grid_spec=pltpu.PrefetchScalarGridSpec(
            num_scalar_prefetch=1,
            grid=(groups,),
            in_specs=[row_spec, row_spec, key_spec, key_spec],
            out_specs=(pl.BlockSpec((2 * HD, rows), lambda g, n: (g, 0)), key_spec, key_spec),
            scratch_shapes=[
                VMEM((prefix, 2 * rows), jnp.float32),
                VMEM((prefix, 2 * rows), jnp.float32),
            ],
        ),
        name="attention_backward",
    )(length, q, d, k, v)


def reduce_kernel(
    w_ref, gq_ref, gk_ref, gv_ref, gi_out, gk_out, gv_out,
    gi_send, gi_recv, gi_own, ring, mine, line,
    gi_sem, ring_send, ring_recv, line_send, line_recv,
):
    z = lax.axis_index("seq_0")
    y = lax.axis_index("seq_1")
    h = lax.axis_index("head")
    right, left = (y + 1) % NY, (y + NY - 1) % NY
    mates = column_mates(z)
    others = ((h + 1) % 3, (h + 2) % 3)
    greet(
        [{"seq_1": right}, {"seq_1": left}]
        + [{"seq_0": m} for m in mates]
        + [{"head": o} for o in others]
    )
    terms = (gk_ref, gv_ref)
    chains = ((0, 1, 4, 0), (1, -1, 4, 4), (0, -1, 3, 8), (1, 1, 3, 11))
    sent = []

    def ring_copy(chain, hop, src):
        kv, way, hops, slot = chain
        i = slot + hop
        return remote(
            src, ring.at[i], ring_send.at[i], ring_recv.at[i], {"seq_1": right if way > 0 else left}
        )

    for chain in chains:
        kv, way, hops, slot = chain
        owner = (y + NY + way * hops) % NY
        copy = ring_copy(chain, 0, terms[kv].at[:, owner])
        copy.start()
        sent.append(copy)

    size = gi_own.shape[0]
    gq = gq_ref[...]
    gi_copies = []
    for i, o in enumerate(others):
        rows = pl.ds(pl.multiple_of(o * size, size), size)
        gi_send[i] = dot_nn(w_ref[rows, :], gq).astype(jnp.bfloat16)
        copy = remote(
            gi_send.at[i], gi_recv.at[i], gi_sem.at[0, i], gi_sem.at[1, i], {"head": o}
        )
        copy.start()
        gi_copies.append(copy)
    gi_own[...] = dot_nn(w_ref[pl.ds(pl.multiple_of(h * size, size), size), :], gq)

    for hop in range(4):
        for chain in chains:
            kv, way, hops, slot = chain
            if hop >= hops:
                continue
            i = slot + hop
            ring_copy(chain, hop, ring.at[i]).wait_recv()
            if hop < hops - 1:
                owner = (y + NY + way * (hops - 1 - hop)) % NY
                ring[i] = (
                    ring[i].astype(jnp.float32) + terms[kv][:, owner].astype(jnp.float32)
                ).astype(jnp.bfloat16)
                copy = ring_copy(chain, hop + 1, ring.at[i])
                copy.start()
                sent.append(copy)
    ends = ((3, 10), (13, 7))
    line_copies = []
    for kv in range(2):
        a, b = ends[kv]
        mine[kv] = (
            ring[a].astype(jnp.float32)
            + ring[b].astype(jnp.float32)
            + terms[kv][:, y].astype(jnp.float32)
        ).astype(jnp.bfloat16)
        for i, m in enumerate(mates):
            copy = remote(
                mine.at[kv, m], line.at[kv, i], line_send.at[kv, i], line_recv.at[kv, i], {"seq_0": m}
            )
            copy.start()
            line_copies.append(copy)
    for i in range(2):
        gi_copies[i].wait_recv()
    gi_out[...] = (
        gi_own[...] + gi_recv[0].astype(jnp.float32) + gi_recv[1].astype(jnp.float32)
    ).astype(jnp.bfloat16)
    for copy in line_copies:
        copy.wait_recv()
    for kv, out in enumerate((gk_out, gv_out)):
        out[...] = (
            mine[kv, z].astype(jnp.float32)
            + line[kv, 0].astype(jnp.float32)
            + line[kv, 1].astype(jnp.float32)
            + line[kv, 2].astype(jnp.float32)
        ).astype(jnp.bfloat16)
    for copy in sent + line_copies + gi_copies:
        copy.wait_send()


def reduced(w, gq, gk, gv):
    features, rows = w.shape[0] // 3, gq.shape[1]
    block = gk.shape[2:]
    return pl.pallas_call(
        reduce_kernel,
        out_shape=(
            jax.ShapeDtypeStruct((features, rows), jnp.bfloat16),
            jax.ShapeDtypeStruct(block, jnp.bfloat16),
            jax.ShapeDtypeStruct(block, jnp.bfloat16),
        ),
        in_specs=[pl.BlockSpec(memory_space=VMEM)] * 4,
        out_specs=(pl.BlockSpec(memory_space=VMEM),) * 3,
        scratch_shapes=[
            VMEM((2, features, rows), jnp.bfloat16),
            VMEM((2, features, rows), jnp.bfloat16),
            VMEM((features, rows), jnp.float32),
            VMEM((14, NZ) + block, jnp.bfloat16),
            VMEM((2, NZ) + block, jnp.bfloat16),
            VMEM((2, 3) + block, jnp.bfloat16),
            DMA((2, 2)),
            DMA((14,)),
            DMA((14,)),
            DMA((2, 3)),
            DMA((2, 3)),
        ],
        compiler_params=pltpu.CompilerParams(collective_id=1, has_side_effects=True),
        name="project_and_reduce",
    )(w, gq, gk, gv)


def on_device(queries, grad_out, keys, values, proj_query, section_span, span_prefix):
    length = span_prefix[section_span[lax.axis_index("section")]].reshape(1)
    k_all, v_all, incoming = gathered(keys[0], values[0], grad_out[0])
    flat = lambda a: a.reshape(-1, a.shape[-1])
    gq, gk, gv = attention(length, queries[0], incoming, flat(k_all), flat(v_all))
    gi, gk, gv = reduced(proj_query[0], gq, gk.reshape(k_all.shape), gv.reshape(v_all.shape))
    return gi[None], gk[None], gv[None]


def solution(mesh):
    split = Mesh(
        mesh.devices.reshape(mesh.shape["section"], NZ, NY, mesh.shape["head"]),
        ("section", "seq_0", "seq_1", "head"),
    )
    in_specs = (
        P("section", SEQ, "head"),
        P("section", SEQ, "head"),
        P("section", SEQ, "head"),
        P("section", SEQ, "head"),
        P("section", None, "head"),
        P(),
        P(),
    )
    out_specs = (P("section", "head", SEQ), P("section", SEQ, "head"), P("section", SEQ, "head"))
    return jax.shard_map(
        on_device, mesh=split, in_specs=in_specs, out_specs=out_specs, check_vma=False
    )
```

time: 329 us -> 133 us (0.40)
  waiting for transfers between devices: 216 us -> 0 us
  Pallas kernels: 0 us -> 122 us
  local copies, waits for them, and re-layouts: 45.7 us -> 7.14 us
  matrix products: 24.5 us -> 0 us
  starting transfers between devices: 17.1 us -> 0 us
  between operations: 15.8 us -> 2.6 us
  other arithmetic: 7.29 us -> 0 us
    all_gather x1 -> x0, waiting for transfers between devices: 130 us -> none  [sent_together(): lax.all_gather(both, axis, axis=dim, tiled=True)]
    pallas_call x0 -> x3, Pallas kernels: none -> 122 us  [the longest x1 66.8 us: reduced(): pl.pallas_call(reduce_kernel, out_shape=(jax.ShapeDtypeStruct((features,...]
    reduce_scatter x2 -> x0, waiting for transfers between devices: 86.5 us -> none  [own_block(): pieces = lax.psum_scatter(pieces, axes[k], scatter_dimension=0, tiled=True)]
    dot_general x19 -> x0, matrix products: 24.5 us -> none  [the longest x3 6.33 us: group_pass(): jnp.dot(dscores, k_group, preferred_element_type=jnp.float32)]
    unnamed x6 -> x3, local copies, waits for them, and re-layouts: 17.1 us -> 4.66 us
    ppermute x1 -> x0, starting transfers between devices: 10.5 us -> none  [shifted(): return lax.ppermute(block, axis, route)]
    split x1 -> x0, local copies, waits for them, and re-layouts: 8.63 us -> none  [sent_together(): jnp.split(lax.all_gather(both, axis, axis=dim, tiled=True), ends, axis=al...]
    all_to_all x1 -> x0, starting transfers between devices: 6.5 us -> none  [sum_at_owner(): lax.all_to_all(pieces, axis, split_axis=0, concat_axis=0, tiled=True)]
  transfers between devices with their start and end apart: 5 -> 0, of which waited for: 3 -> 0; matrix products, arithmetic and copies ran while one was open for 4% -> 0% of each run, Pallas kernels for 0% -> 0%
where the time goes in v1:
time: 133 us; the launch traced here: 131 us
  Pallas kernels  122 us (92%)
  local copies, waits for them, and re-layouts  7.14 us (5%)
  between operations  2.6 us (2%)
    pallas_call x1, Pallas kernels, reduced(): pl.pallas_call(reduce_kernel, out_shape=(jax.ShapeDtypeStruct((features,...  66.8 us
    pallas_call x1, Pallas kernels, gathered(): pl.pallas_call(gather_kernel, out_shape=(jax.ShapeDtypeStruct((NZ, NY) +...  45.4 us
    pallas_call x1, Pallas kernels, attention(): pl.pallas_call(attention_kernel, out_shape=(jax.ShapeDtypeStruct((width,...  9.32 us
    unnamed x3, local copies, waits for them, and re-layouts  4.66 us

profile of v1, /device:TPU:1, one launch (start us, length us, event | category | flops | bytes accessed | tf_op | source)
XLA Modules:
  0.0 131.3 jit_solution(11044968401217184662)
XLA Ops:
  0.6 1.2 dynamic_slice.6
  3.8 1.2 dynamic_slice.7.len_ref
  5.1 45.4 %gather_kv.1 = (bf16[4,8,64,384]{3,2,1,0:T(8,128)(2,1)}, bf16[4,8,64,384]{3,2,1,0:T(8,128)(2,1)}, bf16[128,768]{1,0:T(8,128)(2,1)}) custom-call(bf16[64,384]{1,0:T(8,128)(2,1)} %bitcast.21, bf16[64,384]{1,0:T(8,128)(2,1)} %bitcast.22, bf16[128,768]{1,0:T(8,128)(2,1)} %bitcast.19), custom_call_target="tpu_custom_call" | custom-call | tf_op jit(solution)/shard_map/gather_kv/pallas_call | solution.py:111
  50.5 9.3 %attention_backward.1 = (bf16[768,128]{1,0:T(8,128)(2,1)}, bf16[2048,384]{1,0:T(8,128)(2,1)}, bf16[2048,384]{1,0:T(8,128)(2,1)}) custom-call(s32[1]{0:T(128)} %dynamic_slice.7.len_ref, bf16[128,768]{1,0:T(8,128)(2,1)} %bitcast.20, bf16[128,768]{1,0:T(8,128)(2,1)} %get-tuple-element.12.d_ref, bf16[2048,384]{1,0:T(8,128)(2,1)} %bitcast.14, ...), custom_call_target="tpu_custom_call" | custom-call | tf_op jit(solution)/shard_map/attention_backward/pallas_call | solution.py:187
  59.8 66.8 %project_and_reduce.1 = (bf16[1792,128]{1,0:T(8,128)(2,1)}, bf16[64,384]{1,0:T(8,128)(2,1)}, bf16[64,384]{1,0:T(8,128)(2,1)}) custom-call(bf16[5376,768]{1,0:T(8,128)(2,1)} %bitcast.13, bf16[768,128]{1,0:T(8,128)(2,1)} %get-tuple-element.15.gq_ref, bf16[4,8,64,384]{3,2,1,0:T(8,128)(2,1)} %bitcast.16, bf16[4,8,64,384]{3,2,1,0:T(8,128)(2,1)} %bitcast.17), custom_call_target="tpu_custom_call" | custom-call | tf_op jit(solution)/shard_map/project_and_reduce/pallas_call | solution.py:306
  126.6 1.8 %copy.13 = bf16[1,1792,128]{2,1,0:T(8,128)(2,1)} copy(bf16[1,1792,128]{2,1,0:T(8,128)(2,1)} %bitcast.18) | data formatting | bytes 917504
  128.5 1.4 %copy.14 = bf16[1,64,384]{2,1,0:T(8,128)(2,1)} copy(bf16[1,64,384]{2,1,0:T(8,128)(2,1)} %bitcast.24) | data formatting | bytes 98304
  129.9 1.4 %copy.15 = bf16[1,64,384]{2,1,0:T(8,128)(2,1)} copy(bf16[1,64,384]{2,1,0:T(8,128)(2,1)} %bitcast.23) | data formatting | bytes 98304

commit v2 on v0

v2 whole, which is shorter than its diff:
```python
import functools
import math

import jax
import jax.numpy as jnp
from jax import lax
from jax.experimental import pallas as pl
from jax.experimental.pallas import tpu as pltpu
from jax.sharding import Mesh
from jax.sharding import PartitionSpec as P

HD = 128
SEQ = ("seq_0", "seq_1")
NZ = 4
NY = 8
NS = 8
NH = 3
GROUPS = 3
SCALE = 168.0 ** (-0.5)
SCALE_LOG2 = SCALE * math.log2(math.e)
LEAD = 16
VMEM = pltpu.VMEM
SMEM = pltpu.SMEM
DMA = pltpu.SemaphoreType.DMA
BF16 = jnp.bfloat16
F32 = jnp.float32


def column_mates(z):
    return (z + 1 - 2 * (z % 2), (z + 2) % NZ, NZ - 1 - z)


def remote(src, dst, send, recv, target):
    return pltpu.make_async_remote_copy(
        src_ref=src,
        dst_ref=dst,
        send_sem=send,
        recv_sem=recv,
        device_id=target,
        device_id_type=pl.DeviceIdType.MESH,
    )


def dot_nt(a, b):
    return lax.dot_general(a, b, (((1,), (1,)), ((), ())), preferred_element_type=F32)


def dot_nn(a, b):
    return lax.dot_general(a, b, (((1,), (0,)), ((), ())), preferred_element_type=F32)


def dot_tn(a, b):
    return lax.dot_general(a, b, (((0,), (0,)), ((), ())), preferred_element_type=F32)


def by_eight(x):
    return x.reshape(x.shape[0] // 8, 8, x.shape[1])


def flat(x):
    return x.reshape(x.shape[0] * x.shape[1], x.shape[2])


def tick_kernel(
    span_ref, prefix_ref, q_ref, d_ref, k_ref, v_ref, w_ref,
    gi_out, gk_out, gv_out,
    k_all, v_all, d_new, q2, d2, w_own, w_edge,
    e_buf, dp_buf, stats, ds_buf, p_buf, gk, gv,
    gq, gq_in, gi_send, gi_recv, gi_own, ring, mine, line,
    send, recv_a, recv_b, misc, gq_send, gq_recv, gi_ssem, gi_rsem,
    ring_send, ring_recv, line_send, line_recv,
):
    z = lax.axis_index("seq_0")
    y = lax.axis_index("seq_1")
    h = lax.axis_index("head")
    s = lax.axis_index("section")
    right, left = (y + 1) % NY, (y + NY - 1) % NY
    mates = column_mates(z)
    lower, upper = (s + NS - 1) % NS, (s + 1) % NS
    before, after = (h + NH - 1) % NH, (h + 1) % NH
    top_edge = z // (NZ - 1)
    is_edge = (z % (NZ - 1)) == 0
    goal = (h + NH - 1 + 2 * top_edge) % NH

    w_size = w_own.shape[0]
    w_copies = [
        pltpu.make_async_copy(
            w_ref.at[pl.ds(pl.multiple_of(at * w_size, w_size), w_size), :], buf, misc.at[2 + i]
        )
        for i, (at, buf) in enumerate(((h, w_own), (goal, w_edge)))
    ]
    for copy in w_copies:
        copy.start()

    barrier = pltpu.get_barrier_semaphore()

    def greet(target):
        pl.semaphore_signal(
            barrier, inc=1, device_id=target, device_id_type=pl.DeviceIdType.MESH
        )

    for target in (
        [{"seq_1": right}, {"seq_1": left}]
        + [{"seq_0": m} for m in mates]
        + [{"section": lower}, {"section": upper}]
        + [{"seq_0": z * 0 + NZ - 1, "head": before}, {"seq_0": z * 0, "head": after}]
    ):
        greet(target)

    @pl.when(is_edge)
    def _():
        for j in range(NZ):
            greet({"seq_0": z * 0 + j, "head": goal})

    pl.semaphore_wait(barrier, 9 + 4 * jnp.where(is_edge, 1, 0))

    own = (k_ref, v_ref)
    full = (k_all, v_all)
    size = k_ref.shape[0]
    rows_of = (pl.ds(0, LEAD), pl.ds(LEAD, size - LEAD))
    recv = (recv_a, recv_b)
    sent = []

    def part(kv, cls, z0, y0):
        return full[kv].at[y0, z0, rows_of[cls]]

    def push(src, kv, cls, z0, y0, target):
        copy = remote(
            src, part(kv, cls, z0, y0), send.at[len(sent)], recv[cls].at[kv, y0, z0], target
        )
        copy.start()
        sent.append(copy)

    def arrived(kv, cls, z0, y0):
        block = part(kv, cls, z0, y0)
        remote(block, block, send.at[0], recv[cls].at[kv, y0, z0], {"seq_1": right}).wait_recv()

    both = ({"seq_1": right}, {"seq_1": left})
    for kv in range(2):
        for target in both:
            push(own[kv].at[rows_of[0]], kv, 0, z, y, target)
    for m in mates:
        for kv in range(2):
            push(own[kv].at[rows_of[1]], kv, 1, z, y, {"seq_0": m})
    for kv in range(2):
        for target in both:
            push(own[kv].at[rows_of[1]], kv, 1, z, y, target)
    for m in mates:
        for kv in range(2):
            push(own[kv].at[rows_of[0]], kv, 0, z, y, {"seq_0": m})
    shift = remote(d_ref, d_new, misc.at[0], misc.at[1], {"section": lower})
    shift.start()
    for kv in range(2):
        full[kv][y, z] = own[kv][...]

    length = prefix_ref[span_ref[s]]

    def halves(ref, g):
        return jnp.concatenate(
            [ref[:, 2 * g * HD : (2 * g + 1) * HD], ref[:, (2 * g + 1) * HD : (2 * g + 2) * HD]],
            axis=0,
        )

    for g in range(GROUPS):
        q2[g] = halves(q_ref, g)

    def chunk_of(ref, y0, g):
        return flat(ref[y0, :, :, g * HD : (g + 1) * HD])

    def scores_unit(y0, g):
        sc = dot_nt(chunk_of(k_all, y0, g), q2[g])
        dp = dot_nt(chunk_of(v_all, y0, g), d2[g])
        n = sc.shape[0] // 2
        i = lax.broadcasted_iota(jnp.int32, (n, sc.shape[1]), 0)
        t = i + jnp.where(i >= size, (NY - 1) * size, 0)
        live = t < length - 2 * NY * size - y0 * size
        sc = jnp.concatenate([sc[:n], jnp.where(live, sc[n:], F32(-1e30))], axis=0)
        m = by_eight(sc).max(axis=0).max(axis=0, keepdims=True)
        e = jnp.exp2((sc - m) * SCALE_LOG2)
        e_buf[g, y0] = e
        dp_buf[g, y0] = dp
        stats[0, g, y0] = m
        stats[1, g, y0] = by_eight(e).sum(axis=0).sum(axis=0, keepdims=True)
        stats[2, g, y0] = by_eight(e * dp).sum(axis=0).sum(axis=0, keepdims=True)

    for m in mates:
        for kv in range(2):
            arrived(kv, 1, m, y)
            for target in both:
                push(part(kv, 1, m, y), kv, 1, m, y, target)
    shift.wait_recv()
    for g in range(GROUPS):
        d2[g] = halves(d_new, g)

    reach = ((4, 3), (3, 4))
    todo = [y]
    for hop in range(1, 5):
        y_r, y_l = (y + NY - hop) % NY, (y + hop) % NY
        for kv in range(2):
            for way, y0 in enumerate((y_r, y_l)):
                if hop <= reach[kv][way]:
                    arrived(kv, 0, z, y0)
                    if hop < reach[kv][way]:
                        push(part(kv, 0, z, y0), kv, 0, z, y0, both[way])
                    for m in mates:
                        push(part(kv, 0, z, y0), kv, 0, z, y0, {"seq_0": m})
        units = []
        for y0 in todo:
            for kv in range(2):
                for m in mates:
                    arrived(kv, 0, m, y0)
            units += [(y0, g) for g in range(GROUPS)]
        for m in (z,) + mates:
            for kv in range(2):
                for way, y0 in enumerate((y_r, y_l)):
                    if hop <= reach[kv][way]:
                        arrived(kv, 1, m, y0)
                        if hop < reach[kv][way]:
                            push(part(kv, 1, m, y0), kv, 1, m, y0, both[way])
            for unit in units[:2]:
                scores_unit(*unit)
            units = units[2:]
        todo = [y_r, y_l] if hop < 4 else [y_r]
    for y0 in todo:
        for kv in range(2):
            for m in mates:
                arrived(kv, 0, m, y0)
        for g in range(GROUPS):
            scores_unit(y0, g)

    for g in range(GROUPS):
        m_c = [stats[0, g, c] for c in range(NY)]
        top = functools.reduce(jnp.maximum, m_c)
        f_c = [jnp.exp2((m - top) * SCALE_LOG2) for m in m_c]
        inv = 1.0 / sum(f * stats[1, g, c] for c, f in enumerate(f_c))
        delta = sum(f * stats[2, g, c] for c, f in enumerate(f_c)) * inv
        total = jnp.zeros((HD, q2.shape[1]), F32)
        for c in range(NY):
            p = e_buf[g, c] * (f_c[c] * inv)
            ds = (p * (dp_buf[g, c] - delta)).astype(BF16)
            p_buf[g, c] = p.astype(BF16)
            ds_buf[g, c] = ds
            total = total + dot_tn(chunk_of(k_all, c, g), ds)
        total = (SCALE * total).astype(BF16)
        half = total.shape[1] // 2
        gq[2 * g * HD : (2 * g + 1) * HD, :] = total[:, :half]
        gq[(2 * g + 1) * HD : (2 * g + 2) * HD, :] = total[:, half:]

    def gq_copy(end):
        return remote(
            gq, gq_in.at[z], gq_send.at[end], gq_recv.at[z], {"seq_0": z * 0 + end * (NZ - 1)}
        )

    for end in range(2):
        @pl.when(z != end * (NZ - 1))
        def _():
            gq_copy(end).start()

    for copy in w_copies:
        copy.wait()

    def place(k):
        return k + top_edge * (NZ - 1 - 2 * k)

    def gi_copy(k):
        return remote(
            gi_send.at[k],
            gi_recv.at[1 - top_edge],
            gi_ssem.at[k],
            gi_rsem.at[1 - top_edge],
            {"seq_0": place(k), "head": goal},
        )

    def edge_step(k):
        @pl.when(is_edge)
        def _():
            if k:
                j = place(k)
                remote(
                    gq, gq_in.at[j], gq_send.at[0], gq_recv.at[j], {"seq_0": j}
                ).wait_recv()
                operand = gq_in[j]
            else:
                operand = gq[...]
            gi_send[k] = dot_nn(w_edge[...], operand).astype(BF16)
            gi_copy(k).start()

    edge_step(0)

    terms = (gk, gv)
    chains = ((0, 1, 4, 0), (1, -1, 4, 4), (0, -1, 3, 8), (1, 1, 3, 11))
    ring_sent = []

    def ring_copy(chain, hop, src):
        kv, way, hops, slot = chain
        i = slot + hop
        return remote(src, ring.at[i], ring_send.at[i], ring_recv.at[i], both[0 if way > 0 else 1])

    def terms_unit(y0):
        for g in range(GROUPS):
            cols = slice(g * HD, (g + 1) * HD)
            gk[y0, :, cols] = (SCALE * dot_nn(ds_buf[g, y0], q2[g])).astype(BF16)
            gv[y0, :, cols] = dot_nn(p_buf[g, y0], d2[g]).astype(BF16)

    def ring_start(chain):
        kv, way, hops, slot = chain
        owner = (y + NY + way * hops) % NY
        copy = ring_copy(chain, 0, terms[kv].at[owner])
        copy.start()
        ring_sent.append(copy)

    terms_unit((y + 4) % NY)
    ring_start(chains[0])
    ring_start(chains[1])
    terms_unit((y + 3) % NY)
    ring_start(chains[3])
    terms_unit((y + 5) % NY)
    ring_start(chains[2])
    for d in (2, 6, 1, 7, 0):
        terms_unit((y + d) % NY)
    gi_own[...] = dot_nn(w_own[...], gq[...])

    for hop in range(4):
        if hop < 3:
            edge_step(hop + 1)
        for chain in chains:
            kv, way, hops, slot = chain
            if hop >= hops:
                continue
            i = slot + hop
            ring_copy(chain, hop, ring.at[i]).wait_recv()
            if hop < hops - 1:
                owner = (y + NY + way * (hops - 1 - hop)) % NY
                ring[i] = (ring[i].astype(F32) + terms[kv][owner].astype(F32)).astype(BF16)
                copy = ring_copy(chain, hop + 1, ring.at[i])
                copy.start()
                ring_sent.append(copy)
    ends = ((3, 10), (13, 7))
    line_copies = []
    for kv in range(2):
        a, b = ends[kv]
        mine[kv] = (
            (ring[a].astype(F32) + ring[b].astype(F32) + terms[kv][y].astype(F32))
            .astype(BF16)
            .reshape(mine.shape[1:])
        )
        for i, m in enumerate(mates):
            copy = remote(
                mine.at[kv, m], line.at[kv, i], line_send.at[kv, i], line_recv.at[kv, i], {"seq_0": m}
            )
            copy.start()
            line_copies.append(copy)
    for copy in line_copies:
        copy.wait_recv()
    for kv, out in enumerate((gk_out, gv_out)):
        out[...] = (
            mine[kv, z].astype(F32)
            + line[kv, 0].astype(F32)
            + line[kv, 1].astype(F32)
            + line[kv, 2].astype(F32)
        ).astype(BF16)
    for i in range(2):
        remote(
            gi_send.at[i], gi_recv.at[i], gi_ssem.at[i], gi_rsem.at[i], {"seq_1": right}
        ).wait_recv()
    gi_out[...] = (gi_own[...] + gi_recv[0].astype(F32) + gi_recv[1].astype(F32)).astype(BF16)

    for copy in sent + ring_sent + line_copies:
        copy.wait_send()
    shift.wait_send()
    for end in range(2):
        @pl.when(z != end * (NZ - 1))
        def _():
            gq_copy(end).wait_send()

    @pl.when(is_edge)
    def _():
        for k in range(NZ):
            gi_copy(k).wait_send()


def tick(span, prefix, q, d, k, v, w):
    rows, width = q.shape
    size, kv_width = k.shape
    features = w.shape[0] // NH
    chunk = NZ * size
    block = (NZ, size, kv_width)
    vmem = pl.BlockSpec(memory_space=VMEM)
    return pl.pallas_call(
        tick_kernel,
        out_shape=(
            jax.ShapeDtypeStruct((features, rows), BF16),
            jax.ShapeDtypeStruct(k.shape, BF16),
            jax.ShapeDtypeStruct(v.shape, BF16),
        ),
        in_specs=[pl.BlockSpec(memory_space=SMEM)] * 2
        + [vmem] * 4
        + [pl.BlockSpec(memory_space=pl.ANY)],
        out_specs=(vmem,) * 3,
        scratch_shapes=[
            VMEM((NY,) + block, BF16),
            VMEM((NY,) + block, BF16),
            VMEM((rows, width), BF16),
            VMEM((GROUPS, 2 * rows, HD), BF16),
            VMEM((GROUPS, 2 * rows, HD), BF16),
            VMEM((features, width), BF16),
            VMEM((features, width), BF16),
            VMEM((GROUPS, NY, chunk, 2 * rows), F32),
            VMEM((GROUPS, NY, chunk, 2 * rows), F32),
            VMEM((3, GROUPS, NY, 1, 2 * rows), F32),
            VMEM((GROUPS, NY, chunk, 2 * rows), BF16),
            VMEM((GROUPS, NY, chunk, 2 * rows), BF16),
            VMEM((NY, chunk, kv_width), BF16),
            VMEM((NY, chunk, kv_width), BF16),
            VMEM((width, rows), BF16),
            VMEM((NZ, width, rows), BF16),
            VMEM((NZ, features, rows), BF16),
            VMEM((2, features, rows), BF16),
            VMEM((features, rows), F32),
            VMEM((14, chunk, kv_width), BF16),
            VMEM((2,) + block, BF16),
            VMEM((2, 3, size, kv_width), BF16),
            DMA((124,)),
            DMA((2, NY, NZ)),
            DMA((2, NY, NZ)),
            DMA((4,)),
            DMA((2,)),
            DMA((NZ,)),
            DMA((NZ,)),
            DMA((2,)),
            DMA((14,)),
            DMA((14,)),
            DMA((2, 3)),
            DMA((2, 3)),
        ],
        compiler_params=pltpu.CompilerParams(
            collective_id=0, has_side_effects=True, vmem_limit_bytes=60 * 1024 * 1024
        ),
        name="tick",
    )(span, prefix, q, d, k, v, w)


def hand_on_kernel(*refs):
    for src, dst in zip(refs[:3], refs[3:]):
        dst[...] = src[...]


def hand_on(*arrays):
    vmem = pl.BlockSpec(memory_space=VMEM)
    return pl.pallas_call(
        hand_on_kernel,
        out_shape=tuple(jax.ShapeDtypeStruct(a.shape, a.dtype) for a in arrays),
        in_specs=[vmem] * 3,
        out_specs=(vmem,) * 3,
        name="hand_on",
    )(*arrays)


def on_device(queries, grad_out, keys, values, proj_query, section_span, span_prefix):
    outs = tick(
        section_span, span_prefix, queries[0], grad_out[0], keys[0], values[0], proj_query[0]
    )
    return tuple(a[None] for a in hand_on(*outs))


def solution(mesh):
    split = Mesh(
        mesh.devices.reshape(mesh.shape["section"], NZ, NY, mesh.shape["head"]),
        ("section", "seq_0", "seq_1", "head"),
    )
    in_specs = (
        P("section", SEQ, "head"),
        P("section", SEQ, "head"),
        P("section", SEQ, "head"),
        P("section", SEQ, "head"),
        P("section", None, "head"),
        P(),
        P(),
    )
    out_specs = (P("section", "head", SEQ), P("section", SEQ, "head"), P("section", SEQ, "head"))
    return jax.shard_map(
        on_device, mesh=split, in_specs=in_specs, out_specs=out_specs, check_vma=False
    )
```

time: 329 us -> 112 us (0.34)
  the two profiles are of different devices: /device:TPU:1 before, /device:TPU:4 now
where the time goes in v2:
time: 112 us
  Pallas kernels  111 us (99%)
    pallas_call x1, Pallas kernels, tick(): pl.pallas_call(tick_kernel, out_shape=(jax.ShapeDtypeStruct((features, ro...  109 us

profile of v2, /device:TPU:4, one launch (start us, length us, event | category | flops | bytes accessed | tf_op | source)
XLA Modules:
  0.0 111.8 jit_solution(14503997450578862952)
XLA Ops:
  0.6 109.3 %tick.1 = (bf16[1792,128]{1,0:T(8,128)(2,1)}, bf16[64,384]{1,0:T(8,128)(2,1)}, bf16[64,384]{1,0:T(8,128)(2,1)}) custom-call(s32[8]{0:T(128)} %span_ref.1, s32[8]{0:T(128)} %prefix_ref.1, bf16[128,768]{1,0:T(8,128)(2,1)} %bitcast.9, bf16[128,768]{1,0:T(8,128)(2,1)} %bitcast.10, bf16[64,384]{1,0:T(8,128)(2,1)} %bitcast.11, bf16[64,384]{1,0:T(8,128)(2,1)} %bitcast.12, ...), custom_call_target="tpu_custom_call" | custom-call | tf_op jit(solution)/shard_map/tick/pallas_call | solution.py:389
  110.0 1.9 %hand_on.1 = (bf16[1792,128]{1,0:T(8,128)(2,1)}, bf16[64,384]{1,0:T(8,128)(2,1)}, bf16[64,384]{1,0:T(8,128)(2,1)}) custom-call(bf16[1792,128]{1,0:T(8,128)(2,1)} %get-tuple-element.9.refs_0_, bf16[64,384]{1,0:T(8,128)(2,1)} %get-tuple-element.10.refs_1_, bf16[64,384]{1,0:T(8,128)(2,1)} %get-tuple-element.11.refs_2_), custom_call_target="tpu_custom_call" | custom-call | tf_op jit(solution)/shard_map/hand_on/pallas_call | solution.py:450

commit v3 on v2

--- a/solution.py
+++ b/solution.py
@@ -62,13 +62,13 @@
 
 
 def tick_kernel(
-    span_ref, prefix_ref, q_ref, d_ref, k_ref, v_ref, w_ref,
+    span_ref, prefix_ref, q_hbm, d_ref, k_ref, v_ref, w_ref,
     gi_out, gk_out, gv_out,
-    k_all, v_all, d_new, q2, d2, w_own, w_edge,
+    q_ref, gi_fin, gkv_fin, k_all, v_all, d_new, q2, d2, w_own, w_edge,
     e_buf, dp_buf, stats, ds_buf, p_buf, gk, gv,
     gq, gq_in, gi_send, gi_recv, gi_own, ring, mine, line,
     send, recv_a, recv_b, misc, gq_send, gq_recv, gi_ssem, gi_rsem,
-    ring_send, ring_recv, line_send, line_recv,
+    ring_send, ring_recv, line_send, line_recv, in_sem, out_sem,
 ):
     z = lax.axis_index("seq_0")
     y = lax.axis_index("seq_1")
@@ -82,16 +82,6 @@
     is_edge = (z % (NZ - 1)) == 0
     goal = (h + NH - 1 + 2 * top_edge) % NH
 
-    w_size = w_own.shape[0]
-    w_copies = [
-        pltpu.make_async_copy(
-            w_ref.at[pl.ds(pl.multiple_of(at * w_size, w_size), w_size), :], buf, misc.at[2 + i]
-        )
-        for i, (at, buf) in enumerate(((h, w_own), (goal, w_edge)))
-    ]
-    for copy in w_copies:
-        copy.start()
-
     barrier = pltpu.get_barrier_semaphore()
 
     def greet(target):
@@ -112,10 +102,14 @@
         for j in range(NZ):
             greet({"seq_0": z * 0 + j, "head": goal})
 
-    pl.semaphore_wait(barrier, 9 + 4 * jnp.where(is_edge, 1, 0))
-
     own = (k_ref, v_ref)
     full = (k_all, v_all)
+    in_copies = [pltpu.make_async_copy(own[kv], full[kv].at[y, z], in_sem.at[kv]) for kv in range(2)]
+    in_copies.append(pltpu.make_async_copy(q_hbm, q_ref, in_sem.at[2]))
+    for copy in in_copies:
+        copy.start()
+    pl.semaphore_wait(barrier, 9 + 4 * jnp.where(is_edge, 1, 0))
+
     size = k_ref.shape[0]
     rows_of = (pl.ds(0, LEAD), pl.ds(LEAD, size - LEAD))
     recv = (recv_a, recv_b)
@@ -150,8 +144,17 @@
             push(own[kv].at[rows_of[0]], kv, 0, z, y, {"seq_0": m})
     shift = remote(d_ref, d_new, misc.at[0], misc.at[1], {"section": lower})
     shift.start()
-    for kv in range(2):
-        full[kv][y, z] = own[kv][...]
+    w_size = w_own.shape[0]
+    w_copies = [
+        pltpu.make_async_copy(
+            w_ref.at[pl.ds(pl.multiple_of(at * w_size, w_size), w_size), :], buf, misc.at[2 + i]
+        )
+        for i, (at, buf) in enumerate(((h, w_own), (goal, w_edge)))
+    ]
+    for copy in w_copies:
+        copy.start()
+    for copy in in_copies:
+        copy.wait()
 
     length = prefix_ref[span_ref[s]]
 
@@ -183,50 +186,64 @@
         stats[1, g, y0] = by_eight(e).sum(axis=0).sum(axis=0, keepdims=True)
         stats[2, g, y0] = by_eight(e * dp).sum(axis=0).sum(axis=0, keepdims=True)
 
-    for m in mates:
+    reach = ((4, 3), (3, 4))
+
+    def hop_rows(hop):
+        return (y + NY - hop) % NY, (y + hop) % NY
+
+    def lead_hop(hop):
         for kv in range(2):
-            arrived(kv, 1, m, y)
-            for target in both:
-                push(part(kv, 1, m, y), kv, 1, m, y, target)
-    shift.wait_recv()
-    for g in range(GROUPS):
-        d2[g] = halves(d_new, g)
-
-    reach = ((4, 3), (3, 4))
-    todo = [y]
-    for hop in range(1, 5):
-        y_r, y_l = (y + NY - hop) % NY, (y + hop) % NY
-        for kv in range(2):
-            for way, y0 in enumerate((y_r, y_l)):
+            for way, y0 in enumerate(hop_rows(hop)):
                 if hop <= reach[kv][way]:
                     arrived(kv, 0, z, y0)
                     if hop < reach[kv][way]:
                         push(part(kv, 0, z, y0), kv, 0, z, y0, both[way])
                     for m in mates:
                         push(part(kv, 0, z, y0), kv, 0, z, y0, {"seq_0": m})
-        units = []
-        for y0 in todo:
+
+    def bulk_hop(hop, m):
+        for kv in range(2):
+            for way, y0 in enumerate(hop_rows(hop)):
+                if hop <= reach[kv][way]:
+                    arrived(kv, 1, m, y0)
+                    if hop < reach[kv][way]:
+                        push(part(kv, 1, m, y0), kv, 1, m, y0, both[way])
+
+    def column(m):
+        for kv in range(2):
+            arrived(kv, 1, m, y)
+            for target in both:
+                push(part(kv, 1, m, y), kv, 1, m, y, target)
+
+    def units_of(rows):
+        for y0 in rows:
             for kv in range(2):
                 for m in mates:
                     arrived(kv, 0, m, y0)
-            units += [(y0, g) for g in range(GROUPS)]
-        for m in (z,) + mates:
-            for kv in range(2):
-                for way, y0 in enumerate((y_r, y_l)):
-                    if hop <= reach[kv][way]:
-                        arrived(kv, 1, m, y0)
-                        if hop < reach[kv][way]:
-                            push(part(kv, 1, m, y0), kv, 1, m, y0, both[way])
+        return [(y0, g) for y0 in rows for g in range(GROUPS)]
+
+    for i, m in enumerate(mates):
+        lead_hop(i + 1)
+        bulk_hop(i + 1, z)
+        column(m)
+    shift.wait_recv()
+    for g in range(GROUPS):
+        d2[g] = halves(d_new, g)
+    lead_hop(4)
+    bulk_hop(4, z)
+    todo = [y]
+    for hop in range(1, 5):
+        bulk_hop(hop, mates[0])
+        units = units_of(todo)
+        for m in mates[1:] + (None,):
             for unit in units[:2]:
                 scores_unit(*unit)
             units = units[2:]
-        todo = [y_r, y_l] if hop < 4 else [y_r]
-    for y0 in todo:
-        for kv in range(2):
-            for m in mates:
-                arrived(kv, 0, m, y0)
-        for g in range(GROUPS):
-            scores_unit(y0, g)
+            if m is not None:
+                bulk_hop(hop, m)
+        todo = hop_rows(hop) if hop < 4 else hop_rows(hop)[:1]
+    for unit in units_of(todo):
+        scores_unit(*unit)
 
     for g in range(GROUPS):
         m_c = [stats[0, g, c] for c in range(NY)]
@@ -321,9 +338,9 @@
     gi_own[...] = dot_nn(w_own[...], gq[...])
 
     for hop in range(4):
-        if hop < 3:
-            edge_step(hop + 1)
-        for chain in chains:
+        for at, chain in enumerate(chains):
+            if at == 2 and hop < 3:
+                edge_step(hop + 1)
             kv, way, hops, slot = chain
             if hop >= hops:
                 continue
@@ -352,18 +369,23 @@
             line_copies.append(copy)
     for copy in line_copies:
         copy.wait_recv()
+    out_copies = []
     for kv, out in enumerate((gk_out, gv_out)):
-        out[...] = (
+        gkv_fin[kv] = (
             mine[kv, z].astype(F32)
             + line[kv, 0].astype(F32)
             + line[kv, 1].astype(F32)
             + line[kv, 2].astype(F32)
         ).astype(BF16)
+        out_copies.append(pltpu.make_async_copy(gkv_fin.at[kv], out, out_sem.at[kv]))
+        out_copies[-1].start()
     for i in range(2):
         remote(
             gi_send.at[i], gi_recv.at[i], gi_ssem.at[i], gi_rsem.at[i], {"seq_1": right}
         ).wait_recv()
-    gi_out[...] = (gi_own[...] + gi_recv[0].astype(F32) + gi_recv[1].astype(F32)).astype(BF16)
+    gi_fin[...] = (gi_own[...] + gi_recv[0].astype(F32) + gi_recv[1].astype(F32)).astype(BF16)
+    out_copies.append(pltpu.make_async_copy(gi_fin, gi_out, out_sem.at[2]))
+    out_copies[-1].start()
 
     for copy in sent + ring_sent + line_copies:
         copy.wait_send()
@@ -378,6 +400,9 @@
         for k in range(NZ):
             gi_copy(k).wait_send()
 
+    for copy in out_copies:
+        copy.wait()
+
 
 def tick(span, prefix, q, d, k, v, w):
     rows, width = q.shape
@@ -385,7 +410,6 @@
     features = w.shape[0] // NH
     chunk = NZ * size
     block = (NZ, size, kv_width)
-    vmem = pl.BlockSpec(memory_space=VMEM)
     return pl.pallas_call(
         tick_kernel,
         out_shape=(
@@ -394,10 +418,12 @@
             jax.ShapeDtypeStruct(v.shape, BF16),
         ),
         in_specs=[pl.BlockSpec(memory_space=SMEM)] * 2
-        + [vmem] * 4
-        + [pl.BlockSpec(memory_space=pl.ANY)],
-        out_specs=(vmem,) * 3,
+        + [pl.BlockSpec(memory_space=pl.ANY)] * 5,
+        out_specs=(pl.BlockSpec(memory_space=pl.ANY),) * 3,
         scratch_shapes=[
+            VMEM(q.shape, BF16),
+            VMEM((features, rows), BF16),
+            VMEM((2,) + k.shape, BF16),
             VMEM((NY,) + block, BF16),
             VMEM((NY,) + block, BF16),
             VMEM((rows, width), BF16),
@@ -432,6 +458,8 @@
             DMA((14,)),
             DMA((2, 3)),
             DMA((2, 3)),
+            DMA((3,)),
+            DMA((3,)),
         ],
         compiler_params=pltpu.CompilerParams(
             collective_id=0, has_side_effects=True, vmem_limit_bytes=60 * 1024 * 1024

time: 112 us -> 108 us (0.964)
  the two profiles are of different devices: /device:TPU:4 before, /device:TPU:1 now
where the time goes in v3:
time: 108 us; the launch traced here: 107 us
  Pallas kernels  107 us (99%)
    pallas_call x1, Pallas kernels, tick(): pl.pallas_call(tick_kernel, out_shape=(jax.ShapeDtypeStruct((features, ro...  105 us

profile of v3, /device:TPU:1, one launch (start us, length us, event | category | flops | bytes accessed | tf_op | source)
XLA Modules:
  0.0 107.2 jit_solution(15620631762030878074)
XLA Ops:
  0.6 104.7 %tick.1 = (bf16[1792,128]{1,0:T(8,128)(2,1)}, bf16[64,384]{1,0:T(8,128)(2,1)}, bf16[64,384]{1,0:T(8,128)(2,1)}) custom-call(s32[8]{0:T(128)} %span_ref.1, s32[8]{0:T(128)} %prefix_ref.1, bf16[128,768]{1,0:T(8,128)(2,1)} %bitcast.9, bf16[128,768]{1,0:T(8,128)(2,1)} %bitcast.10, bf16[64,384]{1,0:T(8,128)(2,1)} %bitcast.11, bf16[64,384]{1,0:T(8,128)(2,1)} %bitcast.12, ...), custom_call_target="tpu_custom_call" | custom-call | tf_op jit(solution)/shard_map/tick/pallas_call | solution.py:413
  105.4 1.9 %hand_on.1 = (bf16[1792,128]{1,0:T(8,128)(2,1)}, bf16[64,384]{1,0:T(8,128)(2,1)}, bf16[64,384]{1,0:T(8,128)(2,1)}) custom-call(bf16[1792,128]{1,0:T(8,128)(2,1)} %get-tuple-element.9.refs_0_, bf16[64,384]{1,0:T(8,128)(2,1)} %get-tuple-element.10.refs_1_, bf16[64,384]{1,0:T(8,128)(2,1)} %get-tuple-element.11.refs_2_), custom_call_target="tpu_custom_call" | custom-call | tf_op jit(solution)/shard_map/hand_on/pallas_call | solution.py:478

commit v4 on v3

--- a/solution.py
+++ b/solution.py
@@ -80,7 +80,14 @@
     before, after = (h + NH - 1) % NH, (h + 1) % NH
     top_edge = z // (NZ - 1)
     is_edge = (z % (NZ - 1)) == 0
-    goal = (h + NH - 1 + 2 * top_edge) % NH
+    side = z // 2
+    goal = (h + NH - 1 + 2 * side) % NH
+
+    def place(distance):
+        return distance + top_edge * (NZ - 1 - 2 * distance)
+
+    own_goal = {"seq_0": z, "head": goal}
+    far_goals = [{"seq_0": place(distance), "head": goal} for distance in (2, 3)]
 
     barrier = pltpu.get_barrier_semaphore()
 
@@ -93,14 +100,18 @@
         [{"seq_1": right}, {"seq_1": left}]
         + [{"seq_0": m} for m in mates]
         + [{"section": lower}, {"section": upper}]
-        + [{"seq_0": z * 0 + NZ - 1, "head": before}, {"seq_0": z * 0, "head": after}]
+        + [
+            {"seq_0": z * side + (NZ - 1) * (1 - side), "head": before},
+            {"seq_0": z * (1 - side), "head": after},
+            own_goal,
+        ]
     ):
         greet(target)
 
     @pl.when(is_edge)
     def _():
-        for j in range(NZ):
-            greet({"seq_0": z * 0 + j, "head": goal})
+        for target in far_goals:
+            greet(target)
 
     own = (k_ref, v_ref)
     full = (k_all, v_all)
@@ -108,7 +119,7 @@
     in_copies.append(pltpu.make_async_copy(q_hbm, q_ref, in_sem.at[2]))
     for copy in in_copies:
         copy.start()
-    pl.semaphore_wait(barrier, 9 + 4 * jnp.where(is_edge, 1, 0))
+    pl.semaphore_wait(barrier, 10 + 2 * jnp.where(is_edge, 1, 0))
 
     size = k_ref.shape[0]
     rows_of = (pl.ds(0, LEAD), pl.ds(LEAD, size - LEAD))
@@ -120,10 +131,10 @@
 
     def push(src, kv, cls, z0, y0, target):
         copy = remote(
-            src, part(kv, cls, z0, y0), send.at[len(sent)], recv[cls].at[kv, y0, z0], target
+            src, part(kv, cls, z0, y0), send.at[0], recv[cls].at[kv, y0, z0], target
         )
         copy.start()
-        sent.append(copy)
+        sent.append(LEAD if cls == 0 else size - LEAD)
 
     def arrived(kv, cls, z0, y0):
         block = part(kv, cls, z0, y0)
@@ -268,41 +279,35 @@
             gq, gq_in.at[z], gq_send.at[end], gq_recv.at[z], {"seq_0": z * 0 + end * (NZ - 1)}
         )
 
-    for end in range(2):
-        @pl.when(z != end * (NZ - 1))
-        def _():
-            gq_copy(end).start()
-
+    def gq_leaves(distance):
+        for end in range(2):
+            @pl.when(z == end * (NZ - 1) + distance * (1 - 2 * end))
+            def _():
+                gq_copy(end).start()
+
+    gq_leaves(2)
     for copy in w_copies:
         copy.wait()
-
-    def place(k):
-        return k + top_edge * (NZ - 1 - 2 * k)
 
     def gi_copy(k):
         return remote(
             gi_send.at[k],
-            gi_recv.at[1 - top_edge],
+            gi_recv.at[1 - side],
             gi_ssem.at[k],
-            gi_rsem.at[1 - top_edge],
-            {"seq_0": place(k), "head": goal},
-        )
+            gi_rsem.at[1 - side],
+            far_goals[k - 1] if k else own_goal,
+        )
+
+    gi_send[0] = dot_nn(w_edge[...], gq[...]).astype(BF16)
+    gi_copy(0).start()
 
     def edge_step(k):
         @pl.when(is_edge)
         def _():
-            if k:
-                j = place(k)
-                remote(
-                    gq, gq_in.at[j], gq_send.at[0], gq_recv.at[j], {"seq_0": j}
-                ).wait_recv()
-                operand = gq_in[j]
-            else:
-                operand = gq[...]
-            gi_send[k] = dot_nn(w_edge[...], operand).astype(BF16)
+            j = place(k + 1)
+            remote(gq, gq_in.at[j], gq_send.at[0], gq_recv.at[j], {"seq_0": j}).wait_recv()
+            gi_send[k] = dot_nn(w_edge[...], gq_in[j]).astype(BF16)
             gi_copy(k).start()
-
-    edge_step(0)
 
     terms = (gk, gv)
     chains = ((0, 1, 4, 0), (1, -1, 4, 4), (0, -1, 3, 8), (1, 1, 3, 11))
@@ -335,12 +340,13 @@
     ring_start(chains[2])
     for d in (2, 6, 1, 7, 0):
         terms_unit((y + d) % NY)
+    gq_leaves(3)
     gi_own[...] = dot_nn(w_own[...], gq[...])
 
     for hop in range(4):
         for at, chain in enumerate(chains):
-            if at == 2 and hop < 3:
-                edge_step(hop + 1)
+            if at == 2 and hop in (1, 2):
+                edge_step(hop)
             kv, way, hops, slot = chain
             if hop >= hops:
                 continue
@@ -387,17 +393,22 @@
     out_copies.append(pltpu.make_async_copy(gi_fin, gi_out, out_sem.at[2]))
     out_copies[-1].start()
 
-    for copy in sent + ring_sent + line_copies:
+    gather_rows = sum(n for n in sent) * k_ref.shape[1] // w_ref.shape[1]
+    gather_all = w_ref.at[pl.ds(0, gather_rows), :]
+    remote(gather_all, gather_all, send.at[0], misc.at[1], both[0]).wait_send()
+    for copy in ring_sent + line_copies:
         copy.wait_send()
     shift.wait_send()
     for end in range(2):
-        @pl.when(z != end * (NZ - 1))
+        @pl.when(side != end)
         def _():
             gq_copy(end).wait_send()
 
+    gi_copy(0).wait_send()
+
     @pl.when(is_edge)
     def _():
-        for k in range(NZ):
+        for k in (1, 2):
             gi_copy(k).wait_send()
 
     for copy in out_copies:
@@ -440,19 +451,19 @@
             VMEM((NY, chunk, kv_width), BF16),
             VMEM((width, rows), BF16),
             VMEM((NZ, width, rows), BF16),
-            VMEM((NZ, features, rows), BF16),
+            VMEM((3, features, rows), BF16),
             VMEM((2, features, rows), BF16),
             VMEM((features, rows), F32),
             VMEM((14, chunk, kv_width), BF16),
             VMEM((2,) + block, BF16),
             VMEM((2, 3, size, kv_width), BF16),
-            DMA((124,)),
+            DMA((1,)),
             DMA((2, NY, NZ)),
             DMA((2, NY, NZ)),
             DMA((4,)),
             DMA((2,)),
             DMA((NZ,)),
-            DMA((NZ,)),
+            DMA((3,)),
             DMA((2,)),
             DMA((14,)),
             DMA((14,)),

time: 108 us -> 103 us (0.954)
  Pallas kernels: 107 us -> 102 us
    pallas_call x1, Pallas kernels: 105 us -> 100 us  [tick(): pl.pallas_call(tick_kernel, out_shape=(jax.ShapeDtypeStruct((features, ro...]
where the time goes in v4:
time: 103 us
  Pallas kernels  102 us (99%)
    pallas_call x1, Pallas kernels, tick(): pl.pallas_call(tick_kernel, out_shape=(jax.ShapeDtypeStruct((features, ro...  100 us

profile of v4, /device:TPU:1, one launch (start us, length us, event | category | flops | bytes accessed | tf_op | source)
XLA Modules:
  0.0 102.6 jit_solution(8647619396397864310)
XLA Ops:
  0.6 100.1 %tick.1 = (bf16[1792,128]{1,0:T(8,128)(2,1)}, bf16[64,384]{1,0:T(8,128)(2,1)}, bf16[64,384]{1,0:T(8,128)(2,1)}) custom-call(s32[8]{0:T(128)} %span_ref.1, s32[8]{0:T(128)} %prefix_ref.1, bf16[128,768]{1,0:T(8,128)(2,1)} %bitcast.9, bf16[128,768]{1,0:T(8,128)(2,1)} %bitcast.10, bf16[64,384]{1,0:T(8,128)(2,1)} %bitcast.11, bf16[64,384]{1,0:T(8,128)(2,1)} %bitcast.12, ...), custom_call_target="tpu_custom_call" | custom-call | tf_op jit(solution)/shard_map/tick/pallas_call | solution.py:424
  100.7 1.9 %hand_on.1 = (bf16[1792,128]{1,0:T(8,128)(2,1)}, bf16[64,384]{1,0:T(8,128)(2,1)}, bf16[64,384]{1,0:T(8,128)(2,1)}) custom-call(bf16[1792,128]{1,0:T(8,128)(2,1)} %get-tuple-element.9.refs_0_, bf16[64,384]{1,0:T(8,128)(2,1)} %get-tuple-element.10.refs_1_, bf16[64,384]{1,0:T(8,128)(2,1)} %get-tuple-element.11.refs_2_), custom_call_target="tpu_custom_call" | custom-call | tf_op jit(solution)/shard_map/hand_on/pallas_call | solution.py:489

commit v5 on v4

--- a/solution.py
+++ b/solution.py
@@ -286,6 +286,7 @@
                 gq_copy(end).start()
 
     gq_leaves(2)
+    gq_leaves(3)
     for copy in w_copies:
         copy.wait()
 
@@ -299,7 +300,10 @@
         )
 
     gi_send[0] = dot_nn(w_edge[...], gq[...]).astype(BF16)
-    gi_copy(0).start()
+
+    @pl.when(is_edge)
+    def _():
+        gi_copy(0).start()
 
     def edge_step(k):
         @pl.when(is_edge)
@@ -340,8 +344,12 @@
     ring_start(chains[2])
     for d in (2, 6, 1, 7, 0):
         terms_unit((y + d) % NY)
-    gq_leaves(3)
     gi_own[...] = dot_nn(w_own[...], gq[...])
+
+    @pl.when(jnp.logical_not(is_edge))
+    def _():
+        gi_copy(0).start()
+
 
     for hop in range(4):
         for at, chain in enumerate(chains):

time: 103 us -> 101 us (0.981)
  Pallas kernels: 102 us -> 99.7 us
    pallas_call x1, Pallas kernels: 100 us -> 97.9 us  [tick(): pl.pallas_call(tick_kernel, out_shape=(jax.ShapeDtypeStruct((features, ro...]
where the time goes in v5:
time: 101 us; the launch traced here: 100 us
  Pallas kernels  99.7 us (99%)
    pallas_call x1, Pallas kernels, tick(): pl.pallas_call(tick_kernel, out_shape=(jax.ShapeDtypeStruct((features, ro...  97.9 us

profile of v5, /device:TPU:1, one launch (start us, length us, event | category | flops | bytes accessed | tf_op | source)
XLA Modules:
  0.0 100.4 jit_solution(13546239236895093357)
XLA Ops:
  0.6 97.9 %tick.1 = (bf16[1792,128]{1,0:T(8,128)(2,1)}, bf16[64,384]{1,0:T(8,128)(2,1)}, bf16[64,384]{1,0:T(8,128)(2,1)}) custom-call(s32[8]{0:T(128)} %span_ref.1, s32[8]{0:T(128)} %prefix_ref.1, bf16[128,768]{1,0:T(8,128)(2,1)} %bitcast.9, bf16[128,768]{1,0:T(8,128)(2,1)} %bitcast.10, bf16[64,384]{1,0:T(8,128)(2,1)} %bitcast.11, bf16[64,384]{1,0:T(8,128)(2,1)} %bitcast.12, ...), custom_call_target="tpu_custom_call" | custom-call | tf_op jit(solution)/shard_map/tick/pallas_call | solution.py:432
  98.5 1.9 %hand_on.1 = (bf16[1792,128]{1,0:T(8,128)(2,1)}, bf16[64,384]{1,0:T(8,128)(2,1)}, bf16[64,384]{1,0:T(8,128)(2,1)}) custom-call(bf16[1792,128]{1,0:T(8,128)(2,1)} %get-tuple-element.9.refs_0_, bf16[64,384]{1,0:T(8,128)(2,1)} %get-tuple-element.10.refs_1_, bf16[64,384]{1,0:T(8,128)(2,1)} %get-tuple-element.11.refs_2_), custom_call_target="tpu_custom_call" | custom-call | tf_op jit(solution)/shard_map/hand_on/pallas_call | solution.py:497

commit v6 on v5

--- a/solution.py
+++ b/solution.py
@@ -123,22 +123,24 @@
 
     size = k_ref.shape[0]
     rows_of = (pl.ds(0, LEAD), pl.ds(LEAD, size - LEAD))
-    recv = (recv_a, recv_b)
     sent = []
 
     def part(kv, cls, z0, y0):
         return full[kv].at[y0, z0, rows_of[cls]]
 
     def push(src, kv, cls, z0, y0, target):
-        copy = remote(
-            src, part(kv, cls, z0, y0), send.at[0], recv[cls].at[kv, y0, z0], target
-        )
+        if cls == 0:
+            sem = recv_a.at[1 if "seq_0" in target else 0, kv, y0]
+        else:
+            sem = recv_b.at[kv, y0, z0]
+        copy = remote(src, part(kv, cls, z0, y0), send.at[0], sem, target)
         copy.start()
         sent.append(LEAD if cls == 0 else size - LEAD)
 
     def arrived(kv, cls, z0, y0):
         block = part(kv, cls, z0, y0)
-        remote(block, block, send.at[0], recv[cls].at[kv, y0, z0], {"seq_1": right}).wait_recv()
+        sem = recv_b.at[kv, y0, z0] if cls else recv_a.at[0, kv, y0]
+        remote(block, block, send.at[0], sem, {"seq_1": right}).wait_recv()
 
     both = ({"seq_1": right}, {"seq_1": left})
     for kv in range(2):
@@ -229,8 +231,8 @@
     def units_of(rows):
         for y0 in rows:
             for kv in range(2):
-                for m in mates:
-                    arrived(kv, 0, m, y0)
+                block = full[kv].at[y0, 0, pl.ds(0, 3 * LEAD)]
+                remote(block, block, send.at[0], recv_a.at[1, kv, y0], both[0]).wait_recv()
         return [(y0, g) for y0 in rows for g in range(GROUPS)]
 
     for i, m in enumerate(mates):
@@ -320,7 +322,7 @@
     def ring_copy(chain, hop, src):
         kv, way, hops, slot = chain
         i = slot + hop
-        return remote(src, ring.at[i], ring_send.at[i], ring_recv.at[i], both[0 if way > 0 else 1])
+        return remote(src, ring.at[i], ring_send.at[0], ring_recv.at[i], both[0 if way > 0 else 1])
 
     def terms_unit(y0):
         for g in range(GROUPS):
@@ -377,7 +379,7 @@
         )
         for i, m in enumerate(mates):
             copy = remote(
-                mine.at[kv, m], line.at[kv, i], line_send.at[kv, i], line_recv.at[kv, i], {"seq_0": m}
+                mine.at[kv, m], line.at[kv, i], line_send.at[0], line_recv.at[kv, i], {"seq_0": m}
             )
             copy.start()
             line_copies.append(copy)
@@ -404,8 +406,8 @@
     gather_rows = sum(n for n in sent) * k_ref.shape[1] // w_ref.shape[1]
     gather_all = w_ref.at[pl.ds(0, gather_rows), :]
     remote(gather_all, gather_all, send.at[0], misc.at[1], both[0]).wait_send()
-    for copy in ring_sent + line_copies:
-        copy.wait_send()
+    remote(ring, ring, ring_send.at[0], ring_recv.at[0], both[0]).wait_send()
+    remote(line, line, line_send.at[0], line_recv.at[0, 0], both[0]).wait_send()
     shift.wait_send()
     for end in range(2):
         @pl.when(side != end)
@@ -466,16 +468,16 @@
             VMEM((2,) + block, BF16),
             VMEM((2, 3, size, kv_width), BF16),
             DMA((1,)),
-            DMA((2, NY, NZ)),
+            DMA((2, 2, NY)),
             DMA((2, NY, NZ)),
             DMA((4,)),
             DMA((2,)),
             DMA((NZ,)),
             DMA((3,)),
             DMA((2,)),
+            DMA((1,)),
             DMA((14,)),
-            DMA((14,)),
-            DMA((2, 3)),
+            DMA((1,)),
             DMA((2, 3)),
             DMA((3,)),
             DMA((3,)),

time: 101 us -> 100 us (0.990)
  no operation moved by 1% of the time
where the time goes in v6:
time: 100 us; the launch traced here: 99.9 us
  Pallas kernels  99.3 us (99%)
    pallas_call x1, Pallas kernels, tick(): pl.pallas_call(tick_kernel, out_shape=(jax.ShapeDtypeStruct((features, ro...  97.4 us

profile of v6, /device:TPU:1, one launch (start us, length us, event | category | flops | bytes accessed | tf_op | source)
XLA Modules:
  0.0 99.9 jit_solution(2167490231241354887)
XLA Ops:
  0.6 97.4 %tick.1 = (bf16[1792,128]{1,0:T(8,128)(2,1)}, bf16[64,384]{1,0:T(8,128)(2,1)}, bf16[64,384]{1,0:T(8,128)(2,1)}) custom-call(s32[8]{0:T(128)} %span_ref.1, s32[8]{0:T(128)} %prefix_ref.1, bf16[128,768]{1,0:T(8,128)(2,1)} %bitcast.9, bf16[128,768]{1,0:T(8,128)(2,1)} %bitcast.10, bf16[64,384]{1,0:T(8,128)(2,1)} %bitcast.11, bf16[64,384]{1,0:T(8,128)(2,1)} %bitcast.12, ...), custom_call_target="tpu_custom_call" | custom-call | tf_op jit(solution)/shard_map/tick/pallas_call | solution.py:434
  98.1 1.9 %hand_on.1 = (bf16[1792,128]{1,0:T(8,128)(2,1)}, bf16[64,384]{1,0:T(8,128)(2,1)}, bf16[64,384]{1,0:T(8,128)(2,1)}) custom-call(bf16[1792,128]{1,0:T(8,128)(2,1)} %get-tuple-element.9.refs_0_, bf16[64,384]{1,0:T(8,128)(2,1)} %get-tuple-element.10.refs_1_, bf16[64,384]{1,0:T(8,128)(2,1)} %get-tuple-element.11.refs_2_), custom_call_target="tpu_custom_call" | custom-call | tf_op jit(solution)/shard_map/hand_on/pallas_call | solution.py:499
